TPU v7x, 32 devices: a whole 2x2x4 slice. The times are simulated.
32 devices in a mesh: dp: 8 (over y, x, core), tensor: 4 (over z).
Axes of the slice: x: 2, y: 2, z: 4, core: 2. Of those that a mesh axis runs over, the one named last changes fastest.
Arguments:
- activations: bfloat16 [16, 1024, 1024], P('dp', 'tensor'), may hold values from -6 to 6
- cotangent: bfloat16 [16, 1024, 1024], P('dp', 'tensor'), may hold values from -6 to 6
- attn_gain: float32 [1024], replicated, may hold values from 0.5 to 1.5
- attn_shift: float32 [1024], replicated, may hold values from -2 to 2
- qkv_weight: bfloat16 [1024, 3072], P('dp', 'tensor'), may hold values from -0.1875 to 0.1875
- qkv_bias: float32 [3072], P('tensor'), may hold values from -3 to 3
- out_weight: bfloat16 [1024, 1024], P('dp', 'tensor'), may hold values from -3.5 to 3.5
- out_bias: float32 [1024], replicated, may hold values from -2 to 2
- mlp_gain: float32 [1024], replicated, may hold values from 0.5 to 1.5
- mlp_shift: float32 [1024], replicated, may hold values from -2 to 2
- fc1_weight: bfloat16 [1024, 4096], P('dp', 'tensor'), may hold values from -0.1875 to 0.1875
- fc1_bias: float32 [4096], P('tensor'), may hold values from -3 to 3
- fc2_weight: bfloat16 [1024, 4096], P('dp', 'tensor'), may hold values from -0.09375 to 0.09375
- fc2_bias: float32 [1024], replicated, may hold values from -2 to 2
Outputs:
- output: bfloat16 [16, 1024, 1024], P('dp', 'tensor')
- input_grad: float32 [16, 1024, 1024], P('dp', 'tensor')
- grad_attn_gain: float32 [1024], replicated
- grad_attn_shift: float32 [1024], replicated
- grad_qkv_weight: float32 [1024, 3072], P('dp', 'tensor')
- grad_qkv_bias: float32 [3072], P('tensor')
- grad_out_weight: float32 [1024, 1024], P('dp', 'tensor')
- grad_out_bias: float32 [1024], replicated
- grad_mlp_gain: float32 [1024], replicated
- grad_mlp_shift: float32 [1024], replicated
- grad_fc1_weight: float32 [1024, 4096], P('dp', 'tensor')
- grad_fc1_bias: float32 [4096], P('tensor')
- grad_fc2_weight: float32 [1024, 4096], P('dp', 'tensor')
- grad_fc2_bias: float32 [1024], replicated
All inputs are finite; a program needn't handle non-finite values.
Results may differ from a plain program's by a relative error of at most 0.02.
Values may be sent and summed in bfloat16 or wider, within the bound.
No kernel may reach another device: no remote copies, remote signals or barrier semaphores. Data moves between devices by JAX's collectives and lax.ppermute only.
A program may use at most 192 MiB of HBM per device.

v0:
```python
import math
import jax
import jax.numpy as jnp
from jax import lax
from jax.sharding import PartitionSpec as P

HD = 64
GRID = 16


def norm_rows(values, gain_vec, shift_vec):
    row_mean = jnp.mean(values, axis=-1, keepdims=True)
    centred = values - row_mean
    variance = jnp.mean(centred * centred, axis=-1, keepdims=True)
    return centred * lax.rsqrt(variance + 1e-06) * gain_vec + shift_vec


def rotary_tables(length):
    section = 2 * (HD // 3 // 2)
    half = section // 2
    position = jnp.arange(length)
    frame = (position // (GRID * GRID)).astype(jnp.float32)
    row_pos = (position // GRID % GRID).astype(jnp.float32)
    col_pos = (position % GRID).astype(jnp.float32)
    omega = 1.0 / 10000.0 ** (jnp.arange(half).astype(jnp.float32) / half)
    pieces = [
        jnp.repeat(coordinate[:, None] * omega[None, :], 2, axis=1)
        for coordinate in (frame, row_pos, col_pos)
    ]
    pieces.append(jnp.zeros((length, HD - 3 * section), jnp.float32))
    angles = jnp.concatenate(pieces, axis=1)
    parity = jnp.where(jnp.arange(HD) % 2 == 0, -1.0, 1.0).astype(jnp.float32)
    return (jnp.cos(angles), jnp.sin(angles) * parity)


def pair_swap(values):
    shape = values.shape
    paired = values.reshape(shape[:-1] + (shape[-1] // 2, 2))
    return paired[..., ::-1].reshape(shape)


def contract(left, right, left_dim, right_dim):
    return lax.dot_general(
        left, right, (((left_dim,), (right_dim,)), ((), ())), preferred_element_type=jnp.float32
    )


def exact_gelu(values):
    return jax.nn.gelu(values, approximate=False)


def body(
    activations,
    cotangent,
    attn_gain,
    attn_shift,
    qkv_weight,
    qkv_bias,
    out_weight,
    out_bias,
    mlp_gain,
    mlp_shift,
    fc1_weight,
    fc1_bias,
    fc2_weight,
    fc2_bias,
):
    tensor_size = lax.axis_size("tensor")
    tensor_rank = lax.axis_index("tensor")
    row_count = activations.shape[1]
    width = activations.shape[2]
    length = row_count * tensor_size
    block_rows = min(512, length)
    block_count = length // block_rows
    local_heads = qkv_weight.shape[1] // (3 * HD)
    packed_cols = qkv_weight.shape[1]
    unit_cols = fc1_weight.shape[1]
    factor = 1.0 / math.sqrt(HD)
    cosine, sine = rotary_tables(length)
    cosine = cosine[:, None, :]
    sine = sine[:, None, :]

    def rotate(values):
        return values * cosine + pair_swap(values) * sine

    def rotate_back(values):
        return values * cosine + pair_swap(values * sine)

    def fetch():
        gathered = (
            lax.all_gather(qkv_weight, "dp", axis=0, tiled=True),
            lax.all_gather(out_weight, "dp", axis=0, tiled=True),
            lax.all_gather(fc1_weight, "dp", axis=0, tiled=True),
            lax.all_gather(fc2_weight, "dp", axis=0, tiled=True),
        )
        return (gathered, gathered)

    def seq_gather(values):
        return lax.all_gather(values, "tensor", axis=0, tiled=True)

    def part_sum(values):
        return lax.psum_scatter(
            values.astype(jnp.bfloat16), "tensor", scatter_dimension=0, tiled=True
        ).astype(jnp.float32)

    def grad_gather(values):
        return lax.all_gather(values, "tensor", axis=0, tiled=True)

    def grad_sum(values):
        return lax.psum_scatter(
            values.astype(jnp.bfloat16), "tensor", scatter_dimension=0, tiled=True
        ).astype(jnp.float32)

    def forward(inputs, weights):
        (weight_qkv, weight_out, weight_up, weight_down), (
            whole_qkv,
            whole_out,
            whole_up,
            whole_down,
        ) = weights
        first_all = seq_gather(norm_rows(inputs, attn_gain, attn_shift).astype(jnp.bfloat16))
        packed = (
            jnp.dot(first_all, weight_qkv, preferred_element_type=jnp.float32) + qkv_bias
        ).reshape(length, local_heads, 3, HD)
        query = rotate(packed[:, :, 0]).astype(jnp.bfloat16)
        key_all = rotate(packed[:, :, 1]).astype(jnp.bfloat16)
        value_all = packed[:, :, 2].astype(jnp.bfloat16)
        outputs = []
        log_sums = []
        for block in range(block_count):
            query_block = query[block * block_rows : (block + 1) * block_rows]
            scores = (
                jnp.einsum("qhd,khd->hqk", query_block, key_all, preferred_element_type=jnp.float32)
                * factor
            )
            row_max = jnp.max(scores, axis=-1, keepdims=True)
            expo = jnp.exp(scores - row_max)
            row_total = jnp.sum(expo, axis=-1, keepdims=True)
            weights_low = (expo / row_total).astype(jnp.bfloat16)
            outputs.append(
                jnp.einsum(
                    "hqk,khd->qhd", weights_low, value_all, preferred_element_type=jnp.float32
                )
            )
            log_sums.append(row_max + jnp.log(row_total))
        heads_out = (
            jnp.concatenate(outputs, axis=0).reshape(length, local_heads * HD).astype(jnp.bfloat16)
        )
        log_total = jnp.concatenate(log_sums, axis=1)
        attended = part_sum(contract(heads_out, weight_out, 1, 1))
        resid = inputs + attended + out_bias
        second_all = seq_gather(norm_rows(resid, mlp_gain, mlp_shift).astype(jnp.bfloat16))
        hidden = jnp.dot(second_all, weight_up, preferred_element_type=jnp.float32) + fc1_bias
        act = exact_gelu(hidden).astype(jnp.bfloat16)
        branch = part_sum(contract(act, weight_down, 1, 1))
        result = resid + branch + fc2_bias
        kept = (
            first_all,
            query,
            key_all,
            value_all,
            log_total,
            heads_out,
            heads_out,
            resid,
            second_all,
            hidden,
            act,
        )
        return (result, kept)

    def backward(inputs, grad_low, kept, weights):
        (weight_qkv, weight_out, weight_up, weight_down), (
            whole_qkv,
            whole_out,
            whole_up,
            whole_down,
        ) = weights
        (
            first_all,
            query,
            key_all,
            value_all,
            log_total,
            heads_out,
            heads_rows,
            resid,
            second_all,
            hidden,
            act,
        ) = kept
        grad_top = grad_low.astype(jnp.float32)
        grad_fc2_bias = jnp.sum(grad_top, axis=0)
        grad_all = grad_gather(grad_low)
        grad_fc2_weight = contract(grad_all, act, 0, 0)
        grad_act = jnp.dot(grad_all, weight_down, preferred_element_type=jnp.float32)
        gelu_pull = jax.vjp(exact_gelu, hidden)[1]
        grad_hidden = gelu_pull(grad_act)[0].astype(jnp.bfloat16)
        grad_fc1_bias = jnp.sum(grad_hidden, axis=0, dtype=jnp.float32)
        grad_fc1_weight = contract(second_all, grad_hidden, 0, 0)
        grad_second = grad_sum(contract(grad_hidden, weight_up, 1, 1))
        second_pull = jax.vjp(norm_rows, resid, mlp_gain, mlp_shift)[1]
        grad_resid_norm, grad_mlp_gain, grad_mlp_shift = second_pull(grad_second)
        grad_resid = grad_top + grad_resid_norm
        grad_out_bias = jnp.sum(grad_resid, axis=0)
        resid_low = grad_resid.astype(jnp.bfloat16)
        resid_all = grad_gather(resid_low)
        grad_out_weight = contract(resid_all, heads_out, 0, 0)
        grad_heads = jnp.dot(resid_all, weight_out, preferred_element_type=jnp.float32).astype(
            jnp.bfloat16
        )
        grad_heads = grad_heads.reshape(length, local_heads, HD)
        grad_key = jnp.zeros((length, local_heads, HD), jnp.float32)
        grad_value = jnp.zeros((length, local_heads, HD), jnp.float32)
        query_grads = []
        for block in range(block_count):
            lower = block * block_rows
            upper = lower + block_rows
            query_block = query[lower:upper]
            grad_block = grad_heads[lower:upper]
            scores = (
                jnp.einsum("qhd,khd->hqk", query_block, key_all, preferred_element_type=jnp.float32)
                * factor
            )
            probs = jnp.exp(scores - log_total[:, lower:upper])
            grad_value = grad_value + jnp.einsum(
                "hqk,qhd->khd",
                probs.astype(jnp.bfloat16),
                grad_block,
                preferred_element_type=jnp.float32,
            )
            grad_probs = jnp.einsum(
                "qhd,khd->hqk", grad_block, value_all, preferred_element_type=jnp.float32
            )
            grad_scores = (
                probs * (grad_probs - jnp.sum(probs * grad_probs, axis=-1, keepdims=True))
            ).astype(jnp.bfloat16)
            query_grads.append(
                jnp.einsum("hqk,khd->qhd", grad_scores, key_all, preferred_element_type=jnp.float32)
                * factor
            )
            grad_key = (
                grad_key
                + jnp.einsum(
                    "hqk,qhd->khd", grad_scores, query_block, preferred_element_type=jnp.float32
                )
                * factor
            )
        grad_query = jnp.concatenate(query_grads, axis=0)
        grad_packed = jnp.stack(
            [rotate_back(grad_query), rotate_back(grad_key), grad_value], axis=2
        )
        grad_packed = grad_packed.reshape(length, packed_cols).astype(jnp.bfloat16)
        grad_qkv_bias = jnp.sum(grad_packed, axis=0, dtype=jnp.float32)
        grad_qkv_weight = contract(first_all, grad_packed, 0, 0)
        grad_first = grad_sum(contract(grad_packed, weight_qkv, 1, 1))
        first_pull = jax.vjp(norm_rows, inputs, attn_gain, attn_shift)[1]
        grad_input_norm, grad_attn_gain, grad_attn_shift = first_pull(grad_first)
        input_grad = grad_resid + grad_input_norm
        grads = (
            grad_attn_gain,
            grad_attn_shift,
            grad_qkv_weight,
            grad_qkv_bias,
            grad_out_weight,
            grad_out_bias,
            grad_mlp_gain,
            grad_mlp_shift,
            grad_fc1_weight,
            grad_fc1_bias,
            grad_fc2_weight,
            grad_fc2_bias,
        )
        return (input_grad, grads)

    def per_clip(totals, inputs_pair):
        clip_in, clip_grad = inputs_pair
        forward_weights = fetch()
        result, kept = forward(clip_in.astype(jnp.float32), forward_weights)
        backward_weights = fetch()
        input_grad, grads = backward(clip_in.astype(jnp.float32), clip_grad, kept, backward_weights)
        totals = tuple((left + right for left, right in zip(totals, grads)))
        return (totals, (result.astype(jnp.bfloat16), input_grad))

    out_cols = local_heads * HD
    start_totals = (
        jnp.zeros((width,), jnp.float32),
        jnp.zeros((width,), jnp.float32),
        jnp.zeros((width, packed_cols), jnp.float32),
        jnp.zeros((packed_cols,), jnp.float32),
        jnp.zeros((width, out_cols), jnp.float32),
        jnp.zeros((width,), jnp.float32),
        jnp.zeros((width,), jnp.float32),
        jnp.zeros((width,), jnp.float32),
        jnp.zeros((width, unit_cols), jnp.float32),
        jnp.zeros((unit_cols,), jnp.float32),
        jnp.zeros((width, unit_cols), jnp.float32),
        jnp.zeros((width,), jnp.float32),
    )
    totals, (output, input_grad) = lax.scan(per_clip, start_totals, (activations, cotangent))
    out_grad = totals[4]
    weight_sums = (
        lax.psum_scatter(
            totals[2].astype(jnp.bfloat16), "dp", scatter_dimension=0, tiled=True
        ).astype(jnp.float32),
        lax.psum_scatter(
            out_grad.astype(jnp.bfloat16), "dp", scatter_dimension=0, tiled=True
        ).astype(jnp.float32),
        lax.psum_scatter(
            totals[8].astype(jnp.bfloat16), "dp", scatter_dimension=0, tiled=True
        ).astype(jnp.float32),
        lax.psum_scatter(
            totals[10].astype(jnp.bfloat16), "dp", scatter_dimension=0, tiled=True
        ).astype(jnp.float32),
    )
    qkv_place = lax.dynamic_update_slice_in_dim(
        jnp.zeros((packed_cols * tensor_size,), jnp.float32),
        totals[3],
        tensor_rank * packed_cols,
        0,
    )
    unit_place = lax.dynamic_update_slice_in_dim(
        jnp.zeros((unit_cols * tensor_size,), jnp.float32), totals[9], tensor_rank * unit_cols, 0
    )
    summed = lax.psum(
        (totals[0], totals[1], qkv_place, totals[5], totals[6], totals[7], unit_place, totals[11]),
        ("dp", "tensor"),
    )
    grad_qkv_bias = lax.dynamic_slice_in_dim(summed[2], tensor_rank * packed_cols, packed_cols, 0)
    grad_fc1_bias = lax.dynamic_slice_in_dim(summed[6], tensor_rank * unit_cols, unit_cols, 0)
    return (
        output,
        input_grad,
        summed[0],
        summed[1],
        weight_sums[0],
        grad_qkv_bias,
        weight_sums[1],
        summed[3],
        summed[4],
        summed[5],
        weight_sums[2],
        grad_fc1_bias,
        weight_sums[3],
        summed[7],
    )


def solution(mesh):
    in_specs = (
        P("dp", "tensor", None),
        P("dp", "tensor", None),
        P(),
        P(),
        P("dp", "tensor"),
        P("tensor"),
        P("dp", "tensor"),
        P(),
        P(),
        P(),
        P("dp", "tensor"),
        P("tensor"),
        P("dp", "tensor"),
        P(),
    )
    out_specs = (
        P("dp", "tensor", None),
        P("dp", "tensor", None),
        P(),
        P(),
        P("dp", "tensor"),
        P("tensor"),
        P("dp", "tensor"),
        P(),
        P(),
        P(),
        P("dp", "tensor"),
        P("tensor"),
        P("dp", "tensor"),
        P(),
    )
    return jax.shard_map(body, mesh=mesh, in_specs=in_specs, out_specs=out_specs, check_vma=False)
```

profile of v0, /device:TPU:0, one launch (start us, length us, event | category | flops | bytes accessed | tf_op | source)
XLA Modules:
  0.0 1281.7 jit_solution(289971395987647129)
XLA Ops:
  12.3 1092.1 %while.38 = (s32[]{:T(128)}, f32[1024]{0:T(1024)}, f32[1024]{0:T(1024)}, f32[1024,768]{1,0:T(8,128)}, f32[768]{0:T(1024)}, /*index=5*/f32[1024,256]{1,0:T(8,128)...) while((s32[]{:T(128)}, f32[1024]{0:T(1024)}, ...), condition=%wide.wide.region_27.28_spmd.clone, body=%wide.wide.region_0.27_spmd.clone.sunk | while | flops 22775205888 | bytes 743322112 | solution.py:300
  17.9 14.5 %all_gather.51 = bf16[1024,256]{1,0:T(8,128)(2,1)} all-gather(bf16[128,256]{1,0:T(8,128)(2,1)} %get-tuple-element.931), channel_id=1, replica_groups=mesh['dp'=8,'tensor'=4] {'dp'}, dimensions={0}, use_global_device_ids=true | all-gather | bytes 589824 | tf_op jit(solution)/shard_map/while/body/eval_jaxpr/all_gather | solution.py:92
  32.4 12.2 all-gather.15.cloned.1.call-done
  44.7 47.8 %all-gather.13.cloned.1.call-done = bf16[1024,1024]{1,0:T(8,128)(2,1)} async-done(((bf16[256,1024]{1,0:T(8,128)(2,1)}), bf16[1024,1024]{1,0:T(8,128)(2,1)}) %all-gather.13.cloned.1.call-update) | async-done | bytes 2097168 | tf_op jit(solution)/shard_map/while/body/eval_jaxpr/all_gather | solution.py:99
  99.9 5.3 rev.25
  108.5 5.2 rev.24
  134.9 42.0 %reduce-scatter.17.cloned.1.call-done = bf16[256,1024]{1,0:T(8,128)(2,1)} async-done(((bf16[1024,1024]{1,0:T(8,128)(2,1)}), bf16[256,1024]{1,0:T(8,128)(2,1)}) %reduce-scatter.17.cloned.1.call-update) | async-done | bytes 524304 | tf_op jit(solution)/shard_map/while/body/eval_jaxpr/reduce_scatter | solution.py:102
  183.5 22.1 %all-gather.19.cloned.1.call-done = bf16[1024,1024]{1,0:T(8,128)(2,1)} async-done(((bf16[128,1024]{1,0:T(8,128)(2,1)}), bf16[1024,1024]{1,0:T(8,128)(2,1)}) %all-gather.19.cloned.1.call-update) | async-done | bytes 2097168 | tf_op jit(solution)/shard_map/while/body/eval_jaxpr/all_gather | solution.py:93
  205.6 47.7 %all-gather.17.cloned.1.call-done = bf16[1024,1024]{1,0:T(8,128)(2,1)} async-done(((bf16[256,1024]{1,0:T(8,128)(2,1)}), bf16[1024,1024]{1,0:T(8,128)(2,1)}) %all-gather.17.cloned.1.call-update) | async-done | bytes 2097168 | tf_op jit(solution)/shard_map/while/body/eval_jaxpr/all_gather | solution.py:99
  253.2 15.4 %multiply_convert_fusion.9 = (bf16[1024,1024]{1,0:T(8,128)(2,1)}, f32[1024,1024]{1,0:T(8,128)}, f32[1024,1024]{1,0:T(8,128)}) fusion(f32[1024]{0:T(1024)S(1)} %copy-done.66, bf16[1024,1024]{1,0:T(8,128)(2,1)} %all-gather.17.cloned.1.call-done, bf16[1024,1024]{1,0:T(8,128)(2,1)} %all-gather.19.cloned.1.call-done), kind=kOutput, calls=%fused_computation.22.clone.clone.1 | convolution fusion | flops 2216689664 | bytes 14684160 | tf_op jit(solution)/shard_map/while/body/eval_jaxpr/dot_general | solution.py:153
  268.6 31.1 %all-gather.23.cloned.1.call-done = bf16[1,1024,1024]{2,1,0:T(8,128)(2,1)} async-done(((bf16[1,256,1024]{2,1,0:T(8,128)(2,1)}), bf16[1,1024,1024]{2,1,0:T(8,128)(2,1)}) %all-gather.23.cloned.1.call-update) | async-done | bytes 2097168 | tf_op jit(solution)/shard_map/while/body/eval_jaxpr/all_gather | solution.py:107
  299.7 28.5 %all-gather.21.cloned.1.call-done = bf16[1024,1024]{1,0:T(8,128)(2,1)} async-done(((bf16[128,1024]{1,0:T(8,128)(2,1)}), bf16[1024,1024]{1,0:T(8,128)(2,1)}) %all-gather.21.cloned.1.call-update) | async-done | bytes 2097168 | tf_op jit(solution)/shard_map/while/body/eval_jaxpr/all_gather | solution.py:94
  328.2 8.4 convert_reduce_fusion.18
  341.8 43.7 %reduce-scatter.19.cloned.1.call-done = bf16[256,1024]{1,0:T(8,128)(2,1)} async-done(((bf16[1024,1024]{1,0:T(8,128)(2,1)}), bf16[256,1024]{1,0:T(8,128)(2,1)}) %reduce-scatter.19.cloned.1.call-update) | async-done | bytes 524304 | tf_op jit(solution)/shard_map/while/body/eval_jaxpr/reduce_scatter | solution.py:110
  394.1 6.0 convolution_convert_fusion.19
  400.4 36.9 %all-gather.25.cloned.1.call-done = bf16[1024,1024]{1,0:T(8,128)(2,1)} async-done(((bf16[256,1024]{1,0:T(8,128)(2,1)}), bf16[1024,1024]{1,0:T(8,128)(2,1)}) %all-gather.25.cloned.1.call-update) | async-done | bytes 2097168 | tf_op jit(solution)/shard_map/while/body/eval_jaxpr/all_gather | solution.py:107
  440.3 5.4 multiply_reduce_fusion.18
  451.0 6.1 multiply_reduce_fusion.19
  459.6 7.0 multiply_convert_fusion.11
  486.3 6.3 rev.27
  510.6 6.2 select_add_fusion.37
  530.2 22.9 %reduce-scatter.21.cloned.1.call-done = bf16[256,1024]{1,0:T(8,128)(2,1)} async-done(((bf16[1024,1024]{1,0:T(8,128)(2,1)}), bf16[256,1024]{1,0:T(8,128)(2,1)}) %reduce-scatter.21.cloned.1.call-update) | async-done | bytes 524304 | tf_op jit(solution)/shard_map/while/body/eval_jaxpr/reduce_scatter | solution.py:110
  564.5 11.8 all_gather.51
  576.4 11.2 all-gather.15.cloned.1.call-done
  587.6 47.8 %all-gather.13.cloned.1.call-done = bf16[1024,1024]{1,0:T(8,128)(2,1)} async-done(((bf16[256,1024]{1,0:T(8,128)(2,1)}), bf16[1024,1024]{1,0:T(8,128)(2,1)}) %all-gather.13.cloned.1.call-update) | async-done | bytes 2097168 | tf_op jit(solution)/shard_map/while/body/eval_jaxpr/all_gather | solution.py:99
  642.8 5.3 rev.25
  677.8 41.9 %reduce-scatter.17.cloned.1.call-done = bf16[256,1024]{1,0:T(8,128)(2,1)} async-done(((bf16[1024,1024]{1,0:T(8,128)(2,1)}), bf16[256,1024]{1,0:T(8,128)(2,1)}) %reduce-scatter.17.cloned.1.call-update) | async-done | bytes 524304 | tf_op jit(solution)/shard_map/while/body/eval_jaxpr/reduce_scatter | solution.py:102
  726.2 22.3 %all-gather.19.cloned.1.call-done = bf16[1024,1024]{1,0:T(8,128)(2,1)} async-done(((bf16[128,1024]{1,0:T(8,128)(2,1)}), bf16[1024,1024]{1,0:T(8,128)(2,1)}) %all-gather.19.cloned.1.call-update) | async-done | bytes 2097168 | tf_op jit(solution)/shard_map/while/body/eval_jaxpr/all_gather | solution.py:93
  748.5 47.7 %all-gather.17.cloned.1.call-done = bf16[1024,1024]{1,0:T(8,128)(2,1)} async-done(((bf16[256,1024]{1,0:T(8,128)(2,1)}), bf16[1024,1024]{1,0:T(8,128)(2,1)}) %all-gather.17.cloned.1.call-update) | async-done | bytes 2097168 | tf_op jit(solution)/shard_map/while/body/eval_jaxpr/all_gather | solution.py:99
  796.2 15.4 %multiply_convert_fusion.9 = (bf16[1024,1024]{1,0:T(8,128)(2,1)}, f32[1024,1024]{1,0:T(8,128)}, f32[1024,1024]{1,0:T(8,128)}) fusion(f32[1024]{0:T(1024)S(1)} %copy-done.66, bf16[1024,1024]{1,0:T(8,128)(2,1)} %all-gather.17.cloned.1.call-done, bf16[1024,1024]{1,0:T(8,128)(2,1)} %all-gather.19.cloned.1.call-done), kind=kOutput, calls=%fused_computation.22.clone.clone.1 | convolution fusion | flops 2216689664 | bytes 14684160 | tf_op jit(solution)/shard_map/while/body/eval_jaxpr/dot_general | solution.py:153
  811.6 31.1 %all-gather.23.cloned.1.call-done = bf16[1,1024,1024]{2,1,0:T(8,128)(2,1)} async-done(((bf16[1,256,1024]{2,1,0:T(8,128)(2,1)}), bf16[1,1024,1024]{2,1,0:T(8,128)(2,1)}) %all-gather.23.cloned.1.call-update) | async-done | bytes 2097168 | tf_op jit(solution)/shard_map/while/body/eval_jaxpr/all_gather | solution.py:107
  842.7 28.4 %all-gather.21.cloned.1.call-done = bf16[1024,1024]{1,0:T(8,128)(2,1)} async-done(((bf16[128,1024]{1,0:T(8,128)(2,1)}), bf16[1024,1024]{1,0:T(8,128)(2,1)}) %all-gather.21.cloned.1.call-update) | async-done | bytes 2097168 | tf_op jit(solution)/shard_map/while/body/eval_jaxpr/all_gather | solution.py:94
  871.0 8.4 convert_reduce_fusion.18
  884.6 43.7 %reduce-scatter.19.cloned.1.call-done = bf16[256,1024]{1,0:T(8,128)(2,1)} async-done(((bf16[1024,1024]{1,0:T(8,128)(2,1)}), bf16[256,1024]{1,0:T(8,128)(2,1)}) %reduce-scatter.19.cloned.1.call-update) | async-done | bytes 524304 | tf_op jit(solution)/shard_map/while/body/eval_jaxpr/reduce_scatter | solution.py:110
  936.9 6.0 convolution_convert_fusion.19
  943.2 36.9 %all-gather.25.cloned.1.call-done = bf16[1024,1024]{1,0:T(8,128)(2,1)} async-done(((bf16[256,1024]{1,0:T(8,128)(2,1)}), bf16[1024,1024]{1,0:T(8,128)(2,1)}) %all-gather.25.cloned.1.call-update) | async-done | bytes 2097168 | tf_op jit(solution)/shard_map/while/body/eval_jaxpr/all_gather | solution.py:107
  983.1 5.4 multiply_reduce_fusion.18
  993.8 6.1 multiply_reduce_fusion.19
  1002.5 7.0 multiply_convert_fusion.11
  1029.1 6.3 rev.27
  1053.4 7.4 select_add_fusion.37
  1060.9 6.7 select_add_fusion.39
  1073.1 5.8 select_add_fusion.33
  1078.9 17.0 %reduce-scatter.21.cloned.1.call-done = bf16[256,1024]{1,0:T(8,128)(2,1)} async-done(((bf16[1024,1024]{1,0:T(8,128)(2,1)}), bf16[256,1024]{1,0:T(8,128)(2,1)}) %reduce-scatter.21.cloned.1.call-update) | async-done | bytes 524304 | tf_op jit(solution)/shard_map/while/body/eval_jaxpr/reduce_scatter | solution.py:110
  1118.6 40.9 %all-reduce = (f32[1024]{0:T(1024)}, f32[1024]{0:T(1024)}, f32[3072]{0:T(1024)S(1)}, f32[1024]{0:T(1024)}, f32[1024]{0:T(1024)}, /*index=5*/f32[1024]{0:T(1024)}, f32[4096]{0:T(1024)S(1)}, f32[1024]{0:T(1024)}) all-reduce(f32[1024]{0:T(1024)S(1)} %copy-done.58, ...), channel_id=1, replica_groups=mesh['dp'=8,'tensor'=4] {'dp','tensor'}, use_global_device_ids=true, to_apply=%region_28.29 | all-reduce | flops 13312 | bytes 106496 | tf_op jit(solution)/shard_map/psum | solution.py:325
  1162.3 21.2 %reduce-scatter.9.cloned.1.call-done = bf16[128,768]{1,0:T(8,128)(2,1)} async-done(((bf16[1024,768]{1,0:T(8,128)(2,1)}), bf16[128,768]{1,0:T(8,128)(2,1)}) %reduce-scatter.9.cloned.1.call-update) | async-done | bytes 196624 | tf_op jit(solution)/shard_map/reduce_scatter | solution.py:303
  1185.1 42.5 %reduce-scatter.13.cloned.1.call-done = bf16[128,1024]{1,0:T(8,128)(2,1)} async-done(((bf16[1024,1024]{1,0:T(8,128)(2,1)}), bf16[128,1024]{1,0:T(8,128)(2,1)}) %reduce-scatter.13.cloned.1.call-update) | async-done | bytes 262160 | tf_op jit(solution)/shard_map/reduce_scatter | solution.py:309
  1229.4 42.5 %reduce-scatter.15.cloned.1.call-done = bf16[128,1024]{1,0:T(8,128)(2,1)} async-done(((bf16[1024,1024]{1,0:T(8,128)(2,1)}), bf16[128,1024]{1,0:T(8,128)(2,1)}) %reduce-scatter.15.cloned.1.call-update) | async-done | bytes 262160 | tf_op jit(solution)/shard_map/reduce_scatter | solution.py:312
  (541 shorter events, 272.0 us)
Async XLA Ops:
  12.3 380.0 %copy-start.19 = (f32[1024,1,64]{0,2,1:T(8,128)}, f32[1024,1,64]{0,2,1:T(8,128)S(1)}, u32[]{:S(2)}) copy-start(f32[1024,1,64]{0,2,1:T(8,128)S(1)} %get-tuple-element.928) | copy-start | bytes 786436 | tf_op jit(solution)/shard_map/while
  12.3 32.3 %all-gather.15.cloned.1.call-start = ((), (), s32[]{:S(2)}) async-start(), calls=%async_computation.13 | async-start | bytes 1769472 | tf_op jit(solution)/shard_map/while/body/eval_jaxpr/all_gather | solution.py:91
  13.0 79.4 %all-gather.13.cloned.1.call-start = ((), (), s32[]{:S(2)}) async-start(), calls=%async_computation.12 | async-start | bytes 2621440 | tf_op jit(solution)/shard_map/while/body/eval_jaxpr/all_gather | solution.py:99
  14.3 82.1 %copy-start.35 = (f32[256]{0:T(256)}, f32[256]{0:T(256)S(1)}, u32[]{:S(2)}) copy-start(f32[256]{0:T(256)S(1)} %broadcast_multiply_fusion.16) | copy-start | bytes 3076 | tf_op jit(solution)/shard_map/while
  15.6 80.8 %copy-start.39 = (f32[256]{0:T(256)}, f32[256]{0:T(256)S(1)}, u32[]{:S(2)}) copy-start(f32[256]{0:T(256)S(1)} %fusion.322) | copy-start | bytes 3076 | tf_op jit(solution)/shard_map/while
  15.7 80.8 %copy-start.37 = (f32[256]{0:T(256)}, f32[256]{0:T(256)S(1)}, u32[]{:S(2)}) copy-start(f32[256]{0:T(256)S(1)} %fusion.323) | copy-start | bytes 3076 | tf_op jit(solution)/shard_map/while
  17.8 159.0 %reduce-scatter.17.cloned.1.call-start = ((), (), s32[]{:S(2)}) async-start(), calls=%async_computation.14 | async-start | bytes 2621440 | tf_op jit(solution)/shard_map/while/body/eval_jaxpr/reduce_scatter | solution.py:102
  131.2 45.6 %copy-start.2 = (bf16[2,256,1024]{2,1,0:T(8,128)(2,1)S(1)}, bf16[2,256,1024]{2,1,0:T(8,128)(2,1)}, u32[]{:S(2)}) copy-start(bf16[2,256,1024]{2,1,0:T(8,128)(2,1)} %get-tuple-element.923) | copy-start | bytes 3145732 | tf_op jit(solution)/shard_map/while
  131.2 48.3 %copy-start.34 = (f32[1024]{0:T(1024)S(1)}, f32[1024]{0:T(1024)}, u32[]{:S(2)}) copy-start(f32[1024]{0:T(1024)} %get-tuple-element.933) | copy-start | bytes 12292 | tf_op jit(solution)/shard_map/while
  131.2 48.3 %copy-start.59 = (f32[1024]{0:T(1024)S(1)}, f32[1024]{0:T(1024)}, u32[]{:S(2)}) copy-start(f32[1024]{0:T(1024)} %get-tuple-element.934) | copy-start | bytes 12292 | tf_op jit(solution)/shard_map/while
  132.1 49.7 %copy-start.31 = (bf16[2,256,1024]{2,1,0:T(8,128)(2,1)S(1)}, bf16[2,256,1024]{2,1,0:T(8,128)(2,1)}, u32[]{:S(2)}) copy-start(bf16[2,256,1024]{2,1,0:T(8,128)(2,1)} %get-tuple-element.930) | copy-start | bytes 3145732 | tf_op jit(solution)/shard_map/while
  134.2 119.0 %copy-start.66 = (f32[1024]{0:T(1024)S(1)}, f32[1024]{0:T(1024)}, u32[]{:S(2)}) copy-start(f32[1024]{0:T(1024)} %get-tuple-element.936) | copy-start | bytes 12292 | tf_op jit(solution)/shard_map/while
  134.2 71.3 %all-gather.19.cloned.1.call-start = ((), (), s32[]{:S(2)}) async-start(), calls=%async_computation.16 | async-start | bytes 2359296 | tf_op jit(solution)/shard_map/while/body/eval_jaxpr/all_gather | solution.py:93
  134.8 118.4 %all-gather.17.cloned.1.call-start = ((), (), s32[]{:S(2)}) async-start(), calls=%async_computation.15 | async-start | bytes 2621440 | tf_op jit(solution)/shard_map/while/body/eval_jaxpr/all_gather | solution.py:99
  181.7 118.0 %all-gather.23.cloned.1.call-start = ((), (), s32[]{:S(2)}) async-start(), calls=%async_computation.18 | async-start | bytes 2621440 | tf_op jit(solution)/shard_map/while/body/eval_jaxpr/all_gather | solution.py:107
  182.7 145.6 %all-gather.21.cloned.1.call-start = ((), (), s32[]{:S(2)}) async-start(), calls=%async_computation.17 | async-start | bytes 2359296 | tf_op jit(solution)/shard_map/while/body/eval_jaxpr/all_gather | solution.py:94
  183.4 202.1 %reduce-scatter.19.cloned.1.call-start = ((), (), s32[]{:S(2)}) async-start(), calls=%async_computation.19 | async-start | bytes 2621440 | tf_op jit(solution)/shard_map/while/body/eval_jaxpr/reduce_scatter | solution.py:110
  338.0 47.5 %copy-start.4 = (bf16[256,1024]{1,0:T(8,128)(2,1)S(1)}, bf16[256,1024]{1,0:T(8,128)(2,1)}, u32[]{:S(2)}) copy-start(bf16[256,1024]{1,0:T(8,128)(2,1)} %reduce-scatter.17.cloned.1.call-done) | copy-start | bytes 1572868 | tf_op jit(solution)/shard_map/while
  341.7 47.1 %copy-start.14 = (bf16[1,256,1024]{2,1,0:T(8,128)(2,1)S(1)}, bf16[1,256,1024]{2,1,0:T(8,128)(2,1)}, u32[]{:S(2)}) copy-start(bf16[1,256,1024]{2,1,0:T(8,128)(2,1)} %get-tuple-element.811) | copy-start | bytes 1572868 | tf_op jit(solution)/shard_map/while
  341.7 95.5 %all-gather.25.cloned.1.call-start = ((), (), s32[]{:S(2)}) async-start(), calls=%async_computation.20 | async-start | bytes 2621440 | tf_op jit(solution)/shard_map/while/body/eval_jaxpr/all_gather | solution.py:107
  392.2 129.1 %reduce-scatter.23.cloned.1.call-start = ((), (), s32[]{:S(2)}) async-start(), calls=%async_computation.22 | async-start | bytes 2621440 | tf_op jit(solution)/shard_map/while/body/eval_jaxpr/reduce_scatter | solution.py:102
  400.1 153.0 %reduce-scatter.21.cloned.1.call-start = ((), (), s32[]{:S(2)}) async-start(), calls=%async_computation.21 | async-start | bytes 2621440 | tf_op jit(solution)/shard_map/while/body/eval_jaxpr/reduce_scatter | solution.py:110
  559.1 376.0 %copy-start.19 = (f32[1024,1,64]{0,2,1:T(8,128)}, f32[1024,1,64]{0,2,1:T(8,128)S(1)}, u32[]{:S(2)}) copy-start(f32[1024,1,64]{0,2,1:T(8,128)S(1)} %get-tuple-element.928) | copy-start | bytes 786436 | tf_op jit(solution)/shard_map/while
  559.1 28.5 %all-gather.15.cloned.1.call-start = ((), (), s32[]{:S(2)}) async-start(), calls=%async_computation.13 | async-start | bytes 1769472 | tf_op jit(solution)/shard_map/while/body/eval_jaxpr/all_gather | solution.py:91
  559.7 75.7 %all-gather.13.cloned.1.call-start = ((), (), s32[]{:S(2)}) async-start(), calls=%async_computation.12 | async-start | bytes 2621440 | tf_op jit(solution)/shard_map/while/body/eval_jaxpr/all_gather | solution.py:99
  560.9 78.4 %copy-start.35 = (f32[256]{0:T(256)}, f32[256]{0:T(256)S(1)}, u32[]{:S(2)}) copy-start(f32[256]{0:T(256)S(1)} %broadcast_multiply_fusion.16) | copy-start | bytes 3076 | tf_op jit(solution)/shard_map/while
  562.3 77.1 %copy-start.39 = (f32[256]{0:T(256)}, f32[256]{0:T(256)S(1)}, u32[]{:S(2)}) copy-start(f32[256]{0:T(256)S(1)} %fusion.322) | copy-start | bytes 3076 | tf_op jit(solution)/shard_map/while
  562.3 77.1 %copy-start.37 = (f32[256]{0:T(256)}, f32[256]{0:T(256)S(1)}, u32[]{:S(2)}) copy-start(f32[256]{0:T(256)S(1)} %fusion.323) | copy-start | bytes 3076 | tf_op jit(solution)/shard_map/while
  564.5 155.3 %reduce-scatter.17.cloned.1.call-start = ((), (), s32[]{:S(2)}) async-start(), calls=%async_computation.14 | async-start | bytes 2621440 | tf_op jit(solution)/shard_map/while/body/eval_jaxpr/reduce_scatter | solution.py:102
  674.1 45.6 %copy-start.2 = (bf16[2,256,1024]{2,1,0:T(8,128)(2,1)S(1)}, bf16[2,256,1024]{2,1,0:T(8,128)(2,1)}, u32[]{:S(2)}) copy-start(bf16[2,256,1024]{2,1,0:T(8,128)(2,1)} %get-tuple-element.923) | copy-start | bytes 3145732 | tf_op jit(solution)/shard_map/while
  674.1 48.3 %copy-start.34 = (f32[1024]{0:T(1024)S(1)}, f32[1024]{0:T(1024)}, u32[]{:S(2)}) copy-start(f32[1024]{0:T(1024)} %get-tuple-element.933) | copy-start | bytes 12292 | tf_op jit(solution)/shard_map/while
  674.1 48.3 %copy-start.59 = (f32[1024]{0:T(1024)S(1)}, f32[1024]{0:T(1024)}, u32[]{:S(2)}) copy-start(f32[1024]{0:T(1024)} %get-tuple-element.934) | copy-start | bytes 12292 | tf_op jit(solution)/shard_map/while
  675.0 49.7 %copy-start.31 = (bf16[2,256,1024]{2,1,0:T(8,128)(2,1)S(1)}, bf16[2,256,1024]{2,1,0:T(8,128)(2,1)}, u32[]{:S(2)}) copy-start(bf16[2,256,1024]{2,1,0:T(8,128)(2,1)} %get-tuple-element.930) | copy-start | bytes 3145732 | tf_op jit(solution)/shard_map/while
  677.1 119.1 %copy-start.66 = (f32[1024]{0:T(1024)S(1)}, f32[1024]{0:T(1024)}, u32[]{:S(2)}) copy-start(f32[1024]{0:T(1024)} %get-tuple-element.936) | copy-start | bytes 12292 | tf_op jit(solution)/shard_map/while
  677.2 71.3 %all-gather.19.cloned.1.call-start = ((), (), s32[]{:S(2)}) async-start(), calls=%async_computation.16 | async-start | bytes 2359296 | tf_op jit(solution)/shard_map/while/body/eval_jaxpr/all_gather | solution.py:93
  677.8 118.4 %all-gather.17.cloned.1.call-start = ((), (), s32[]{:S(2)}) async-start(), calls=%async_computation.15 | async-start | bytes 2621440 | tf_op jit(solution)/shard_map/while/body/eval_jaxpr/all_gather | solution.py:99
  724.7 118.0 %all-gather.23.cloned.1.call-start = ((), (), s32[]{:S(2)}) async-start(), calls=%async_computation.18 | async-start | bytes 2621440 | tf_op jit(solution)/shard_map/while/body/eval_jaxpr/all_gather | solution.py:107
  725.6 145.4 %all-gather.21.cloned.1.call-start = ((), (), s32[]{:S(2)}) async-start(), calls=%async_computation.17 | async-start | bytes 2359296 | tf_op jit(solution)/shard_map/while/body/eval_jaxpr/all_gather | solution.py:94
  726.2 202.1 %reduce-scatter.19.cloned.1.call-start = ((), (), s32[]{:S(2)}) async-start(), calls=%async_computation.19 | async-start | bytes 2621440 | tf_op jit(solution)/shard_map/while/body/eval_jaxpr/reduce_scatter | solution.py:110
  880.8 47.5 %copy-start.4 = (bf16[256,1024]{1,0:T(8,128)(2,1)S(1)}, bf16[256,1024]{1,0:T(8,128)(2,1)}, u32[]{:S(2)}) copy-start(bf16[256,1024]{1,0:T(8,128)(2,1)} %reduce-scatter.17.cloned.1.call-done) | copy-start | bytes 1572868 | tf_op jit(solution)/shard_map/while
  884.5 47.1 %copy-start.14 = (bf16[1,256,1024]{2,1,0:T(8,128)(2,1)S(1)}, bf16[1,256,1024]{2,1,0:T(8,128)(2,1)}, u32[]{:S(2)}) copy-start(bf16[1,256,1024]{2,1,0:T(8,128)(2,1)} %get-tuple-element.811) | copy-start | bytes 1572868 | tf_op jit(solution)/shard_map/while
  884.5 95.5 %all-gather.25.cloned.1.call-start = ((), (), s32[]{:S(2)}) async-start(), calls=%async_computation.20 | async-start | bytes 2621440 | tf_op jit(solution)/shard_map/while/body/eval_jaxpr/all_gather | solution.py:107
  935.0 132.7 %reduce-scatter.23.cloned.1.call-start = ((), (), s32[]{:S(2)}) async-start(), calls=%async_computation.22 | async-start | bytes 2621440 | tf_op jit(solution)/shard_map/while/body/eval_jaxpr/reduce_scatter | solution.py:102
  942.9 153.0 %reduce-scatter.21.cloned.1.call-start = ((), (), s32[]{:S(2)}) async-start(), calls=%async_computation.21 | async-start | bytes 2621440 | tf_op jit(solution)/shard_map/while/body/eval_jaxpr/reduce_scatter | solution.py:110
  1104.5 56.3 %reduce-scatter.11.cloned.1.call-start = ((), (), s32[]{:S(2)}) async-start(), calls=%async_computation.9 | async-start | bytes 589824 | tf_op jit(solution)/shard_map/reduce_scatter | solution.py:306
  1106.6 76.8 %reduce-scatter.9.cloned.1.call-start = ((), (), s32[]{:S(2)}) async-start(), calls=%async_computation.8 | async-start | bytes 1769472 | tf_op jit(solution)/shard_map/reduce_scatter | solution.py:303
  1109.9 117.7 %reduce-scatter.13.cloned.1.call-start = ((), (), s32[]{:S(2)}) async-start(), calls=%async_computation.10 | async-start | bytes 2359296 | tf_op jit(solution)/shard_map/reduce_scatter | solution.py:309
  1113.8 158.1 %reduce-scatter.15.cloned.1.call-start = ((), (), s32[]{:S(2)}) async-start(), calls=%async_computation.11 | async-start | bytes 2359296 | tf_op jit(solution)/shard_map/reduce_scatter | solution.py:312
  (122 other events, 1000.8 us)
Sparse Core Ops, SparseCore 0:
  15.0 29.6 all-gather.14
  46.8 45.6 all-gather.12
  134.3 42.4 reduce-scatter.16
  178.6 26.9 all-gather.18
  207.5 45.6 all-gather.16
  255.2 44.4 all-gather.22
  301.6 26.5 all-gather.20
  341.8 43.6 reduce-scatter.18
  392.4 44.8 all-gather.24
  439.4 42.4 reduce-scatter.22
  510.6 42.4 reduce-scatter.20
  561.5 26.0 all-gather.14
  589.7 45.6 all-gather.12
  677.3 42.4 reduce-scatter.16
  721.5 26.9 all-gather.18
  750.5 45.6 all-gather.16
  798.2 44.4 all-gather.22
  844.4 26.5 all-gather.20
  884.7 43.6 reduce-scatter.18
  935.2 44.8 all-gather.24
  982.4 42.4 reduce-scatter.22
  1053.4 42.4 reduce-scatter.20
Sparse Core Ops, SparseCore 1:
  1108.6 33.3 reduce-scatter.10
  1145.2 38.2 reduce-scatter.8
  1186.6 41.0 reduce-scatter.12
  1230.9 41.0 reduce-scatter.14
where the time goes:
time: 1290 us; the launch traced here: 1280 us
  waiting for transfers between devices  773 us (60%)
  matrix products  199 us (15%)
  other arithmetic  115 us (9%)
  local copies, waits for them, and re-layouts  104 us (8%)
  blocking collectives  67.2 us (5%)
  between operations  16.3 us (1%)
    all_gather x4, waiting for transfers between devices, seq_gather(): return lax.all_gather(values, 'tensor', axis=0, tiled=True)  191 us
    all_gather x4, waiting for transfers between devices, grad_gather(): return lax.all_gather(values, 'tensor', axis=0, tiled=True)  136 us
    reduce_scatter x4, waiting for transfers between devices, grad_sum(): lax.psum_scatter(values.astype(jnp.bfloat16), 'tensor', scatter_dimension...  127 us
    reduce_scatter x4, waiting for transfers between devices, part_sum(): lax.psum_scatter(values.astype(jnp.bfloat16), 'tensor', scatter_dimension...  83.9 us
    dot_general x16, matrix products, contract(): lax.dot_general(left, right, (((left_dim,), (right_dim,)), ((), ())), pre...  69.9 us
    all_gather x2, waiting for transfers between devices, fetch(): lax.all_gather(fc2_weight, 'dp', axis=0, tiled=True)  56.9 us
    all_gather x2, waiting for transfers between devices, fetch(): lax.all_gather(fc1_weight, 'dp', axis=0, tiled=True)  44.4 us
    reduce_scatter x1, waiting for transfers between devices, body(): lax.psum_scatter(totals[10].astype(jnp.bfloat16), 'dp', scatter_dimension...  42.5 us
  transfers between devices with their start and end apart: 26, of which 23 were waited for; matrix products, arithmetic and copies ran while one was open for 21% of the time, Pallas kernels for 0%

commit v1 on v0

--- a/solution.py
+++ b/solution.py
@@ -6,6 +6,19 @@
 
 HD = 64
 GRID = 16
+
+
+def ring_gather(value, axis, dim):
+    ways = lax.axis_size(axis)
+    up = [(d, (d + 1) % ways) for d in range(ways)]
+    down = [(d, (d - 1) % ways) for d in range(ways)]
+    earlier, later = ([value], [value])
+    for _ in range(ways // 2):
+        earlier.append(lax.ppermute(earlier[-1], axis, up))
+    for _ in range((ways - 1) // 2):
+        later.append(lax.ppermute(later[-1], axis, down))
+    line = jnp.concatenate([*earlier[::-1], *later[1:]], axis=dim)
+    return jnp.roll(line, (lax.axis_index(axis) - ways // 2) * value.shape[dim], axis=dim)
 
 
 def norm_rows(values, gain_vec, shift_vec):
@@ -104,7 +117,7 @@
         ).astype(jnp.float32)
 
     def grad_gather(values):
-        return lax.all_gather(values, "tensor", axis=0, tiled=True)
+        return ring_gather(values, "tensor", 0)
 
     def grad_sum(values):
         return lax.psum_scatter(

time: 1290 us -> 1200 us (0.930)
  waiting for transfers between devices: 773 us -> 600 us
  other arithmetic: 115 us -> 163 us
  starting transfers between devices: 1.42 us -> 47.4 us
    all_gather x4 -> x0, waiting for transfers between devices: 136 us -> none  [grad_gather(): return lax.all_gather(values, 'tensor', axis=0, tiled=True)]
    ppermute x0 -> x12, waiting for transfers between devices: none -> 95.8 us  [the longest x8 94.6 us: ring_gather(): earlier.append(lax.ppermute(earlier[-1], axis, up))]
    all_gather x4, waiting for transfers between devices: 191 us -> 137 us  [seq_gather(): return lax.all_gather(values, 'tensor', axis=0, tiled=True)]
    concatenate x0 -> x4, other arithmetic: none -> 48.1 us  [ring_gather(): jnp.roll(line, (lax.axis_index(axis) - ways // 2) * value.shape[dim], axi...]
    ppermute x0 -> x12, starting transfers between devices: none -> 46 us  [the longest x8 33.3 us: ring_gather(): earlier.append(lax.ppermute(earlier[-1], axis, up))]
    all_gather x2, waiting for transfers between devices: 44.4 us -> 0.01 us  [fetch(): lax.all_gather(fc1_weight, 'dp', axis=0, tiled=True)]
    all_gather x2, waiting for transfers between devices: 56.9 us -> 25.3 us  [fetch(): lax.all_gather(fc2_weight, 'dp', axis=0, tiled=True)]
  transfers between devices with their start and end apart: 26 -> 34, of which waited for: 23 -> 27; matrix products, arithmetic and copies ran while one was open for 21% -> 26% of each run, Pallas kernels for 0% -> 0%
where the time goes in v1:
time: 1200 us; the launch traced here: 1190 us
  waiting for transfers between devices  600 us (50%)
  matrix products  192 us (16%)
  other arithmetic  163 us (14%)
  local copies, waits for them, and re-layouts  103 us (9%)
  blocking collectives  67.3 us (6%)
  starting transfers between devices  47.4 us (4%)
  between operations  16.2 us (1%)
    all_gather x4, waiting for transfers between devices, seq_gather(): return lax.all_gather(values, 'tensor', axis=0, tiled=True)  137 us
    reduce_scatter x4, waiting for transfers between devices, grad_sum(): lax.psum_scatter(values.astype(jnp.bfloat16), 'tensor', scatter_dimension...  126 us
    ppermute x8, waiting for transfers between devices, ring_gather(): earlier.append(lax.ppermute(earlier[-1], axis, up))  94.6 us
    reduce_scatter x4, waiting for transfers between devices, part_sum(): lax.psum_scatter(values.astype(jnp.bfloat16), 'tensor', scatter_dimension...  83.8 us
    dot_general x16, matrix products, contract(): lax.dot_general(left, right, (((left_dim,), (right_dim,)), ((), ())), pre...  65.4 us
    concatenate x4, other arithmetic, ring_gather(): jnp.roll(line, (lax.axis_index(axis) - ways // 2) * value.shape[dim], axi...  48.1 us
    reduce_scatter x1, waiting for transfers between devices, body(): lax.psum_scatter(totals[10].astype(jnp.bfloat16), 'dp', scatter_dimension...  42.5 us
    reduce_scatter x1, waiting for transfers between devices, body(): lax.psum_scatter(totals[8].astype(jnp.bfloat16), 'dp', scatter_dimension=...  42.5 us
  transfers between devices with their start and end apart: 34, of which 27 were waited for; matrix products, arithmetic and copies ran while one was open for 26% of the time, Pallas kernels for 0%

profile of v1, /device:TPU:0, one launch (start us, length us, event | category | flops | bytes accessed | tf_op | source)
XLA Modules:
  0.0 1194.7 jit_solution(18387007358626220348)
XLA Ops:
  12.3 1005.3 %while.40 = (s32[]{:T(128)}, f32[1024]{0:T(1024)}, f32[1024]{0:T(1024)}, f32[1024,768]{1,0:T(8,128)}, f32[768]{0:T(1024)}, /*index=5*/f32[1024,256]{1,0:T(8,128)...) while((s32[]{:T(128)}, f32[1024]{0:T(1024)}, ...), condition=%wide.wide.region_27.29_spmd.clone, body=%wide.wide.region_0.28_spmd.clone.sunk | while | flops 22808760320 | bytes 767505216 | solution.py:313
  17.9 14.5 %all_gather.60 = bf16[1024,256]{1,0:T(8,128)(2,1)} all-gather(bf16[128,256]{1,0:T(8,128)(2,1)} %get-tuple-element.1164), channel_id=1, replica_groups=mesh['dp'=8,'tensor'=4] {'dp'}, dimensions={0}, use_global_device_ids=true | all-gather | bytes 589824 | tf_op jit(solution)/shard_map/while/body/eval_jaxpr/all_gather | solution.py:105
  32.4 12.2 %all-gather.8.cloned.1.call-done = bf16[1024,768]{1,0:T(8,128)(2,1)} async-done(((bf16[128,768]{1,0:T(8,128)(2,1)}), bf16[1024,768]{1,0:T(8,128)(2,1)}) %all-gather.8.cloned.1.call-update) | async-done | bytes 1572880 | tf_op jit(solution)/shard_map/while/body/eval_jaxpr/all_gather | solution.py:104
  44.7 47.8 %all-gather.6.cloned.1.call-done = bf16[1024,1024]{1,0:T(8,128)(2,1)} async-done(((bf16[256,1024]{1,0:T(8,128)(2,1)}), bf16[1024,1024]{1,0:T(8,128)(2,1)}) %all-gather.6.cloned.1.call-update) | async-done | bytes 2097168 | tf_op jit(solution)/shard_map/while/body/eval_jaxpr/all_gather | solution.py:112
  134.9 42.0 %reduce-scatter.17.cloned.1.call-done = bf16[256,1024]{1,0:T(8,128)(2,1)} async-done(((bf16[1024,1024]{1,0:T(8,128)(2,1)}), bf16[256,1024]{1,0:T(8,128)(2,1)}) %reduce-scatter.17.cloned.1.call-update) | async-done | bytes 524304 | tf_op jit(solution)/shard_map/while/body/eval_jaxpr/reduce_scatter | solution.py:115
  186.9 12.8 %collective-permute-done = bf16[256,1024]{1,0:T(8,128)(2,1)S(1)} collective-permute-done((bf16[256,1024]{1,0:T(8,128)(2,1)S(1)}, bf16[256,1024]{1,0:T(8,128)(2,1)S(1)}, u32[]{:S(2)}, u32[]{:S(2)}) %collective-permute-start) | collective-permute-done | bytes 524320 | tf_op jit(solution)/shard_map/while/body/eval_jaxpr/ppermute | solution.py:17
  199.6 7.6 collective-permute-start.1
  208.2 14.0 %collective-permute-done.1 = bf16[256,1024]{1,0:T(8,128)(2,1)} collective-permute-done((bf16[256,1024]{1,0:T(8,128)(2,1)S(1)}, bf16[256,1024]{1,0:T(8,128)(2,1)}, u32[]{:S(2)}, u32[]{:S(2)}) %collective-permute-start.1) | collective-permute-done | bytes 524320 | tf_op jit(solution)/shard_map/while/body/eval_jaxpr/ppermute | solution.py:17
  222.2 12.5 %fusion.346 = bf16[1024,1024]{1,0:T(8,128)(2,1)} fusion(s32[]{:T(128)S(6)} %select_n.113, bf16[256,1024]{1,0:T(8,128)(2,1)} %collective-permute-done.1, bf16[256,1024]{1,0:T(8,128)(2,1)S(1)} %collective-permute-done, bf16[256,1024]{1,0:T(8,128)(2,1)S(1)} %get-tuple-element.1033, bf16[256,1024]{1,0:T(8,128)(2,1)S(1)} %collective-permute-done.2), kind=kLoop, calls=%fused_computation.73.clone.clone.1 | loop fusion | flops 16777216 | bytes 4194308 | tf_op jit(solution)/shard_map/while/body/eval_jaxpr/jit(_roll_dynamic)/concatenate | solution.py:21
  234.7 20.5 %all-gather.10.cloned.1.call-done = bf16[1024,1024]{1,0:T(8,128)(2,1)} async-done(((bf16[256,1024]{1,0:T(8,128)(2,1)}), bf16[1024,1024]{1,0:T(8,128)(2,1)}) %all-gather.10.cloned.1.call-update) | async-done | bytes 2097168 | tf_op jit(solution)/shard_map/while/body/eval_jaxpr/all_gather | solution.py:112
  255.2 15.4 %multiply_convert_fusion.9 = (bf16[1024,1024]{1,0:T(8,128)(2,1)}, f32[1024,1024]{1,0:T(8,128)}, f32[1024,1024]{1,0:T(8,128)}) fusion(f32[1024]{0:T(1024)S(1)} %copy-done.72, bf16[1024,1024]{1,0:T(8,128)(2,1)} %all-gather.10.cloned.1.call-done, bf16[1024,1024]{1,0:T(8,128)(2,1)} %all-gather.12.cloned.1.call-done), kind=kOutput, calls=%fused_computation.38.clone.clone.1 | convolution fusion | flops 2216689664 | bytes 14684160 | tf_op jit(solution)/shard_map/while/body/eval_jaxpr/dot_general | solution.py:166
  270.6 12.7 %all-gather.14.cloned.1.call-done = bf16[1024,1024]{1,0:T(8,128)(2,1)} async-done(((bf16[128,1024]{1,0:T(8,128)(2,1)}), bf16[1024,1024]{1,0:T(8,128)(2,1)}) %all-gather.14.cloned.1.call-update) | async-done | bytes 2097168 | tf_op jit(solution)/shard_map/while/body/eval_jaxpr/all_gather | solution.py:107
  283.2 8.4 convert_reduce_fusion.18
  296.8 43.7 %reduce-scatter.19.cloned.1.call-done = bf16[256,1024]{1,0:T(8,128)(2,1)} async-done(((bf16[1024,1024]{1,0:T(8,128)(2,1)}), bf16[256,1024]{1,0:T(8,128)(2,1)}) %reduce-scatter.19.cloned.1.call-update) | async-done | bytes 524304 | tf_op jit(solution)/shard_map/while/body/eval_jaxpr/reduce_scatter | solution.py:123
  352.3 10.9 collective-permute-done.3
  363.3 7.6 collective-permute-start.4
  374.7 9.7 collective-permute-done.4
  384.4 11.6 fusion.349
  416.6 7.1 multiply_convert_fusion.11
  443.4 6.2 rev.39
  487.4 22.1 %reduce-scatter.21.cloned.1.call-done = bf16[256,1024]{1,0:T(8,128)(2,1)} async-done(((bf16[1024,1024]{1,0:T(8,128)(2,1)}), bf16[256,1024]{1,0:T(8,128)(2,1)}) %reduce-scatter.21.cloned.1.call-update) | async-done | bytes 524304 | tf_op jit(solution)/shard_map/while/body/eval_jaxpr/reduce_scatter | solution.py:123
  521.0 11.8 all_gather.60
  532.8 11.3 all-gather.8.cloned.1.call-done
  544.1 47.8 %all-gather.6.cloned.1.call-done = bf16[1024,1024]{1,0:T(8,128)(2,1)} async-done(((bf16[256,1024]{1,0:T(8,128)(2,1)}), bf16[1024,1024]{1,0:T(8,128)(2,1)}) %all-gather.6.cloned.1.call-update) | async-done | bytes 2097168 | tf_op jit(solution)/shard_map/while/body/eval_jaxpr/all_gather | solution.py:112
  634.5 41.8 %reduce-scatter.17.cloned.1.call-done = bf16[256,1024]{1,0:T(8,128)(2,1)} async-done(((bf16[1024,1024]{1,0:T(8,128)(2,1)}), bf16[256,1024]{1,0:T(8,128)(2,1)}) %reduce-scatter.17.cloned.1.call-update) | async-done | bytes 524304 | tf_op jit(solution)/shard_map/while/body/eval_jaxpr/reduce_scatter | solution.py:115
  686.3 12.8 %collective-permute-done = bf16[256,1024]{1,0:T(8,128)(2,1)S(1)} collective-permute-done((bf16[256,1024]{1,0:T(8,128)(2,1)S(1)}, bf16[256,1024]{1,0:T(8,128)(2,1)S(1)}, u32[]{:S(2)}, u32[]{:S(2)}) %collective-permute-start) | collective-permute-done | bytes 524320 | tf_op jit(solution)/shard_map/while/body/eval_jaxpr/ppermute | solution.py:17
  699.1 7.6 collective-permute-start.1
  707.6 13.8 %collective-permute-done.1 = bf16[256,1024]{1,0:T(8,128)(2,1)} collective-permute-done((bf16[256,1024]{1,0:T(8,128)(2,1)S(1)}, bf16[256,1024]{1,0:T(8,128)(2,1)}, u32[]{:S(2)}, u32[]{:S(2)}) %collective-permute-start.1) | collective-permute-done | bytes 524320 | tf_op jit(solution)/shard_map/while/body/eval_jaxpr/ppermute | solution.py:17
  721.4 12.5 %fusion.346 = bf16[1024,1024]{1,0:T(8,128)(2,1)} fusion(s32[]{:T(128)S(6)} %select_n.113, bf16[256,1024]{1,0:T(8,128)(2,1)} %collective-permute-done.1, bf16[256,1024]{1,0:T(8,128)(2,1)S(1)} %collective-permute-done, bf16[256,1024]{1,0:T(8,128)(2,1)S(1)} %get-tuple-element.1033, bf16[256,1024]{1,0:T(8,128)(2,1)S(1)} %collective-permute-done.2), kind=kLoop, calls=%fused_computation.73.clone.clone.1 | loop fusion | flops 16777216 | bytes 4194308 | tf_op jit(solution)/shard_map/while/body/eval_jaxpr/jit(_roll_dynamic)/concatenate | solution.py:21
  733.9 20.7 %all-gather.10.cloned.1.call-done = bf16[1024,1024]{1,0:T(8,128)(2,1)} async-done(((bf16[256,1024]{1,0:T(8,128)(2,1)}), bf16[1024,1024]{1,0:T(8,128)(2,1)}) %all-gather.10.cloned.1.call-update) | async-done | bytes 2097168 | tf_op jit(solution)/shard_map/while/body/eval_jaxpr/all_gather | solution.py:112
  754.6 15.4 %multiply_convert_fusion.9 = (bf16[1024,1024]{1,0:T(8,128)(2,1)}, f32[1024,1024]{1,0:T(8,128)}, f32[1024,1024]{1,0:T(8,128)}) fusion(f32[1024]{0:T(1024)S(1)} %copy-done.72, bf16[1024,1024]{1,0:T(8,128)(2,1)} %all-gather.10.cloned.1.call-done, bf16[1024,1024]{1,0:T(8,128)(2,1)} %all-gather.12.cloned.1.call-done), kind=kOutput, calls=%fused_computation.38.clone.clone.1 | convolution fusion | flops 2216689664 | bytes 14684160 | tf_op jit(solution)/shard_map/while/body/eval_jaxpr/dot_general | solution.py:166
  770.0 12.6 %all-gather.14.cloned.1.call-done = bf16[1024,1024]{1,0:T(8,128)(2,1)} async-done(((bf16[128,1024]{1,0:T(8,128)(2,1)}), bf16[1024,1024]{1,0:T(8,128)(2,1)}) %all-gather.14.cloned.1.call-update) | async-done | bytes 2097168 | tf_op jit(solution)/shard_map/while/body/eval_jaxpr/all_gather | solution.py:107
  782.6 8.4 convert_reduce_fusion.18
  796.2 43.7 %reduce-scatter.19.cloned.1.call-done = bf16[256,1024]{1,0:T(8,128)(2,1)} async-done(((bf16[1024,1024]{1,0:T(8,128)(2,1)}), bf16[256,1024]{1,0:T(8,128)(2,1)}) %reduce-scatter.19.cloned.1.call-update) | async-done | bytes 524304 | tf_op jit(solution)/shard_map/while/body/eval_jaxpr/reduce_scatter | solution.py:123
  851.8 10.9 collective-permute-done.3
  862.7 7.6 collective-permute-start.4
  874.1 9.7 collective-permute-done.4
  883.8 11.6 fusion.349
  907.3 6.2 multiply_reduce_fusion.19
  916.0 7.1 multiply_convert_fusion.11
  942.8 6.2 rev.39
  967.1 7.3 select_add_fusion.39
  974.5 6.9 select_add_fusion.37
  992.5 16.4 %reduce-scatter.21.cloned.1.call-done = bf16[256,1024]{1,0:T(8,128)(2,1)} async-done(((bf16[1024,1024]{1,0:T(8,128)(2,1)}), bf16[256,1024]{1,0:T(8,128)(2,1)}) %reduce-scatter.21.cloned.1.call-update) | async-done | bytes 524304 | tf_op jit(solution)/shard_map/while/body/eval_jaxpr/reduce_scatter | solution.py:123
  1031.8 41.0 %all-reduce = (f32[1024]{0:T(1024)}, f32[1024]{0:T(1024)}, f32[3072]{0:T(1024)S(1)}, f32[1024]{0:T(1024)}, f32[1024]{0:T(1024)}, /*index=5*/f32[1024]{0:T(1024)}, f32[4096]{0:T(1024)S(1)}, f32[1024]{0:T(1024)}) all-reduce(f32[1024]{0:T(1024)S(1)} %copy-done.64, ...), channel_id=1, replica_groups=mesh['dp'=8,'tensor'=4] {'dp','tensor'}, use_global_device_ids=true, to_apply=%region_28.30 | all-reduce | flops 13312 | bytes 106496 | tf_op jit(solution)/shard_map/psum | solution.py:338
  1075.5 21.1 %reduce-scatter.9.cloned.1.call-done = bf16[128,768]{1,0:T(8,128)(2,1)} async-done(((bf16[1024,768]{1,0:T(8,128)(2,1)}), bf16[128,768]{1,0:T(8,128)(2,1)}) %reduce-scatter.9.cloned.1.call-update) | async-done | bytes 196624 | tf_op jit(solution)/shard_map/reduce_scatter | solution.py:316
  1098.3 42.5 %reduce-scatter.13.cloned.1.call-done = bf16[128,1024]{1,0:T(8,128)(2,1)} async-done(((bf16[1024,1024]{1,0:T(8,128)(2,1)}), bf16[128,1024]{1,0:T(8,128)(2,1)}) %reduce-scatter.13.cloned.1.call-update) | async-done | bytes 262160 | tf_op jit(solution)/shard_map/reduce_scatter | solution.py:322
  1142.6 42.5 %reduce-scatter.15.cloned.1.call-done = bf16[128,1024]{1,0:T(8,128)(2,1)} async-done(((bf16[1024,1024]{1,0:T(8,128)(2,1)}), bf16[128,1024]{1,0:T(8,128)(2,1)}) %reduce-scatter.15.cloned.1.call-update) | async-done | bytes 262160 | tf_op jit(solution)/shard_map/reduce_scatter | solution.py:325
  (581 shorter events, 336.0 us)
Async XLA Ops:
  12.3 335.0 %copy-start.19 = (f32[1024,1,64]{0,2,1:T(8,128)}, f32[1024,1,64]{0,2,1:T(8,128)S(1)}, u32[]{:S(2)}) copy-start(f32[1024,1,64]{0,2,1:T(8,128)S(1)} %get-tuple-element.1161) | copy-start | bytes 786436 | tf_op jit(solution)/shard_map/while
  12.3 32.3 %all-gather.8.cloned.1.call-start = ((), (), s32[]{:S(2)}) async-start(), calls=%async_computation.13 | async-start | bytes 1769472 | tf_op jit(solution)/shard_map/while/body/eval_jaxpr/all_gather | solution.py:104
  13.1 79.4 %all-gather.6.cloned.1.call-start = ((), (), s32[]{:S(2)}) async-start(), calls=%async_computation.12 | async-start | bytes 2621440 | tf_op jit(solution)/shard_map/while/body/eval_jaxpr/all_gather | solution.py:112
  14.3 82.1 %copy-start.35 = (f32[256]{0:T(256)}, f32[256]{0:T(256)S(1)}, u32[]{:S(2)}) copy-start(f32[256]{0:T(256)S(1)} %broadcast_multiply_fusion.16) | copy-start | bytes 3076 | tf_op jit(solution)/shard_map/while
  15.7 80.8 %copy-start.39 = (f32[256]{0:T(256)}, f32[256]{0:T(256)S(1)}, u32[]{:S(2)}) copy-start(f32[256]{0:T(256)S(1)} %fusion.335) | copy-start | bytes 3076 | tf_op jit(solution)/shard_map/while
  15.7 80.8 %copy-start.37 = (f32[256]{0:T(256)}, f32[256]{0:T(256)S(1)}, u32[]{:S(2)}) copy-start(f32[256]{0:T(256)S(1)} %fusion.336) | copy-start | bytes 3076 | tf_op jit(solution)/shard_map/while
  17.9 159.0 %reduce-scatter.17.cloned.1.call-start = ((), (), s32[]{:S(2)}) async-start(), calls=%async_computation.14 | async-start | bytes 2621440 | tf_op jit(solution)/shard_map/while/body/eval_jaxpr/reduce_scatter | solution.py:115
  131.3 48.3 %copy-start.34 = (f32[1024]{0:T(1024)S(1)}, f32[1024]{0:T(1024)}, u32[]{:S(2)}) copy-start(f32[1024]{0:T(1024)} %get-tuple-element.1166) | copy-start | bytes 12292 | tf_op jit(solution)/shard_map/while
  131.3 48.3 %copy-start.65 = (f32[1024]{0:T(1024)S(1)}, f32[1024]{0:T(1024)}, u32[]{:S(2)}) copy-start(f32[1024]{0:T(1024)} %get-tuple-element.1167) | copy-start | bytes 12292 | tf_op jit(solution)/shard_map/while
  134.3 100.4 %all-gather.12.cloned.1.call-start = ((), (), s32[]{:S(2)}) async-start(), calls=%async_computation.16 | async-start | bytes 2359296 | tf_op jit(solution)/shard_map/while/body/eval_jaxpr/all_gather | solution.py:106
  134.9 120.3 %all-gather.10.cloned.1.call-start = ((), (), s32[]{:S(2)}) async-start(), calls=%async_computation.15 | async-start | bytes 2621440 | tf_op jit(solution)/shard_map/while/body/eval_jaxpr/all_gather | solution.py:112
  178.2 77.0 %copy-start.72 = (f32[1024]{0:T(1024)S(1)}, f32[1024]{0:T(1024)}, u32[]{:S(2)}) copy-start(f32[1024]{0:T(1024)} %get-tuple-element.1169) | copy-start | bytes 12292 | tf_op jit(solution)/shard_map/while
  181.8 101.4 %all-gather.14.cloned.1.call-start = ((), (), s32[]{:S(2)}) async-start(), calls=%async_computation.17 | async-start | bytes 2359296 | tf_op jit(solution)/shard_map/while/body/eval_jaxpr/all_gather | solution.py:107
  183.0 16.6 %collective-permute-start = (bf16[256,1024]{1,0:T(8,128)(2,1)S(1)}, bf16[256,1024]{1,0:T(8,128)(2,1)S(1)}, u32[]{:S(2)}, u32[]{:S(2)}) collective-permute-start(bf16[256,1024]{1,0:T(8,128)(2,1)S(1)} %get-tuple-element.1033), channel_id=1, source_target_pairs={{0,1},{1,2},{2,3},{3,0},{4,5},{5,6},{6,7},{7,4},{8,9},{9,10},{10,1... | collective-permute-start | bytes 1572872 | tf_op jit(solution)/shard_map/while/body/eval_jaxpr/ppermute | solution.py:17
  183.7 24.5 %collective-permute-start.2 = (bf16[256,1024]{1,0:T(8,128)(2,1)S(1)}, bf16[256,1024]{1,0:T(8,128)(2,1)S(1)}, u32[]{:S(2)}, u32[]{:S(2)}) collective-permute-start(bf16[256,1024]{1,0:T(8,128)(2,1)S(1)} %get-tuple-element.1033), channel_id=1, source_target_pairs={{0,3},{1,0},{2,1},{3,2},{4,7},{5,4},{6,5},{7,6},{8,11},{9,8},{10,9... | collective-permute-start | bytes 1572872 | tf_op jit(solution)/shard_map/while/body/eval_jaxpr/ppermute | solution.py:19
  199.6 22.6 %collective-permute-start.1 = (bf16[256,1024]{1,0:T(8,128)(2,1)S(1)}, bf16[256,1024]{1,0:T(8,128)(2,1)}, u32[]{:S(2)}, u32[]{:S(2)}) collective-permute-start(bf16[256,1024]{1,0:T(8,128)(2,1)S(1)} %collective-permute-done), channel_id=1, source_target_pairs={{0,1},{1,2},{2,3},{3,0},{4,5},{5,6},{6,7},{7,4},{8,9},{9,10},{10,1... | collective-permute-start | bytes 1572872 | tf_op jit(solution)/shard_map/while/body/eval_jaxpr/ppermute | solution.py:17
  207.3 133.2 %reduce-scatter.19.cloned.1.call-start = ((), (), s32[]{:S(2)}) async-start(), calls=%async_computation.18 | async-start | bytes 2621440 | tf_op jit(solution)/shard_map/while/body/eval_jaxpr/reduce_scatter | solution.py:123
  296.8 181.8 %reduce-scatter.23.cloned.1.call-start = ((), (), s32[]{:S(2)}) async-start(), calls=%async_computation.20 | async-start | bytes 2621440 | tf_op jit(solution)/shard_map/while/body/eval_jaxpr/reduce_scatter | solution.py:115
  346.6 16.7 %collective-permute-start.3 = (bf16[256,1024]{1,0:T(8,128)(2,1)S(1)}, bf16[256,1024]{1,0:T(8,128)(2,1)S(1)}, u32[]{:S(2)}, u32[]{:S(2)}) collective-permute-start(bf16[256,1024]{1,0:T(8,128)(2,1)S(1)} %convert_element_type.591), channel_id=1, source_target_pairs={{0,1},{1,2},{2,3},{3,0},{4,5},{5,6},{6,7},{7,4},{8,9},{9,10},{10,1... | collective-permute-start | bytes 1572872 | tf_op jit(solution)/shard_map/while/body/eval_jaxpr/ppermute | solution.py:17
  349.1 25.6 %collective-permute-start.5 = (bf16[256,1024]{1,0:T(8,128)(2,1)S(1)}, bf16[256,1024]{1,0:T(8,128)(2,1)S(1)}, u32[]{:S(2)}, u32[]{:S(2)}) collective-permute-start(bf16[256,1024]{1,0:T(8,128)(2,1)S(1)} %convert_element_type.591), channel_id=1, source_target_pairs={{0,3},{1,0},{2,1},{3,2},{4,7},{5,4},{6,5},{7,6},{8,11},{9,8},{10,9... | collective-permute-start | bytes 1572872 | tf_op jit(solution)/shard_map/while/body/eval_jaxpr/ppermute | solution.py:19
  363.3 21.1 %collective-permute-start.4 = (bf16[256,1024]{1,0:T(8,128)(2,1)S(1)}, bf16[256,1024]{1,0:T(8,128)(2,1)}, u32[]{:S(2)}, u32[]{:S(2)}) collective-permute-start(bf16[256,1024]{1,0:T(8,128)(2,1)S(1)} %collective-permute-done.3), channel_id=1, source_target_pairs={{0,1},{1,2},{2,3},{3,0},{4,5},{5,6},{6,7},{7,4},{8,9},{9,10},{10,1... | collective-permute-start | bytes 1572872 | tf_op jit(solution)/shard_map/while/body/eval_jaxpr/ppermute | solution.py:17
  374.7 134.9 %reduce-scatter.21.cloned.1.call-start = ((), (), s32[]{:S(2)}) async-start(), calls=%async_computation.19 | async-start | bytes 2621440 | tf_op jit(solution)/shard_map/while/body/eval_jaxpr/reduce_scatter | solution.py:123
  515.5 331.1 %copy-start.19 = (f32[1024,1,64]{0,2,1:T(8,128)}, f32[1024,1,64]{0,2,1:T(8,128)S(1)}, u32[]{:S(2)}) copy-start(f32[1024,1,64]{0,2,1:T(8,128)S(1)} %get-tuple-element.1161) | copy-start | bytes 786436 | tf_op jit(solution)/shard_map/while
  515.6 28.5 %all-gather.8.cloned.1.call-start = ((), (), s32[]{:S(2)}) async-start(), calls=%async_computation.13 | async-start | bytes 1769472 | tf_op jit(solution)/shard_map/while/body/eval_jaxpr/all_gather | solution.py:104
  516.1 75.8 %all-gather.6.cloned.1.call-start = ((), (), s32[]{:S(2)}) async-start(), calls=%async_computation.12 | async-start | bytes 2621440 | tf_op jit(solution)/shard_map/while/body/eval_jaxpr/all_gather | solution.py:112
  517.4 78.5 %copy-start.35 = (f32[256]{0:T(256)}, f32[256]{0:T(256)S(1)}, u32[]{:S(2)}) copy-start(f32[256]{0:T(256)S(1)} %broadcast_multiply_fusion.16) | copy-start | bytes 3076 | tf_op jit(solution)/shard_map/while
  518.7 77.1 %copy-start.39 = (f32[256]{0:T(256)}, f32[256]{0:T(256)S(1)}, u32[]{:S(2)}) copy-start(f32[256]{0:T(256)S(1)} %fusion.335) | copy-start | bytes 3076 | tf_op jit(solution)/shard_map/while
  518.8 77.1 %copy-start.37 = (f32[256]{0:T(256)}, f32[256]{0:T(256)S(1)}, u32[]{:S(2)}) copy-start(f32[256]{0:T(256)S(1)} %fusion.336) | copy-start | bytes 3076 | tf_op jit(solution)/shard_map/while
  520.9 155.4 %reduce-scatter.17.cloned.1.call-start = ((), (), s32[]{:S(2)}) async-start(), calls=%async_computation.14 | async-start | bytes 2621440 | tf_op jit(solution)/shard_map/while/body/eval_jaxpr/reduce_scatter | solution.py:115
  630.7 48.3 %copy-start.34 = (f32[1024]{0:T(1024)S(1)}, f32[1024]{0:T(1024)}, u32[]{:S(2)}) copy-start(f32[1024]{0:T(1024)} %get-tuple-element.1166) | copy-start | bytes 12292 | tf_op jit(solution)/shard_map/while
  630.7 48.3 %copy-start.65 = (f32[1024]{0:T(1024)S(1)}, f32[1024]{0:T(1024)}, u32[]{:S(2)}) copy-start(f32[1024]{0:T(1024)} %get-tuple-element.1167) | copy-start | bytes 12292 | tf_op jit(solution)/shard_map/while
  633.7 100.1 %all-gather.12.cloned.1.call-start = ((), (), s32[]{:S(2)}) async-start(), calls=%async_computation.16 | async-start | bytes 2359296 | tf_op jit(solution)/shard_map/while/body/eval_jaxpr/all_gather | solution.py:106
  634.5 120.1 %all-gather.10.cloned.1.call-start = ((), (), s32[]{:S(2)}) async-start(), calls=%async_computation.15 | async-start | bytes 2621440 | tf_op jit(solution)/shard_map/while/body/eval_jaxpr/all_gather | solution.py:112
  677.6 77.0 %copy-start.72 = (f32[1024]{0:T(1024)S(1)}, f32[1024]{0:T(1024)}, u32[]{:S(2)}) copy-start(f32[1024]{0:T(1024)} %get-tuple-element.1169) | copy-start | bytes 12292 | tf_op jit(solution)/shard_map/while
  681.2 101.4 %all-gather.14.cloned.1.call-start = ((), (), s32[]{:S(2)}) async-start(), calls=%async_computation.17 | async-start | bytes 2359296 | tf_op jit(solution)/shard_map/while/body/eval_jaxpr/all_gather | solution.py:107
  682.4 16.6 %collective-permute-start = (bf16[256,1024]{1,0:T(8,128)(2,1)S(1)}, bf16[256,1024]{1,0:T(8,128)(2,1)S(1)}, u32[]{:S(2)}, u32[]{:S(2)}) collective-permute-start(bf16[256,1024]{1,0:T(8,128)(2,1)S(1)} %get-tuple-element.1033), channel_id=1, source_target_pairs={{0,1},{1,2},{2,3},{3,0},{4,5},{5,6},{6,7},{7,4},{8,9},{9,10},{10,1... | collective-permute-start | bytes 1572872 | tf_op jit(solution)/shard_map/while/body/eval_jaxpr/ppermute | solution.py:17
  683.1 24.5 %collective-permute-start.2 = (bf16[256,1024]{1,0:T(8,128)(2,1)S(1)}, bf16[256,1024]{1,0:T(8,128)(2,1)S(1)}, u32[]{:S(2)}, u32[]{:S(2)}) collective-permute-start(bf16[256,1024]{1,0:T(8,128)(2,1)S(1)} %get-tuple-element.1033), channel_id=1, source_target_pairs={{0,3},{1,0},{2,1},{3,2},{4,7},{5,4},{6,5},{7,6},{8,11},{9,8},{10,9... | collective-permute-start | bytes 1572872 | tf_op jit(solution)/shard_map/while/body/eval_jaxpr/ppermute | solution.py:19
  699.1 22.3 %collective-permute-start.1 = (bf16[256,1024]{1,0:T(8,128)(2,1)S(1)}, bf16[256,1024]{1,0:T(8,128)(2,1)}, u32[]{:S(2)}, u32[]{:S(2)}) collective-permute-start(bf16[256,1024]{1,0:T(8,128)(2,1)S(1)} %collective-permute-done), channel_id=1, source_target_pairs={{0,1},{1,2},{2,3},{3,0},{4,5},{5,6},{6,7},{7,4},{8,9},{9,10},{10,1... | collective-permute-start | bytes 1572872 | tf_op jit(solution)/shard_map/while/body/eval_jaxpr/ppermute | solution.py:17
  706.7 133.3 %reduce-scatter.19.cloned.1.call-start = ((), (), s32[]{:S(2)}) async-start(), calls=%async_computation.18 | async-start | bytes 2621440 | tf_op jit(solution)/shard_map/while/body/eval_jaxpr/reduce_scatter | solution.py:123
  796.2 185.3 %reduce-scatter.23.cloned.1.call-start = ((), (), s32[]{:S(2)}) async-start(), calls=%async_computation.20 | async-start | bytes 2621440 | tf_op jit(solution)/shard_map/while/body/eval_jaxpr/reduce_scatter | solution.py:115
  846.0 16.7 %collective-permute-start.3 = (bf16[256,1024]{1,0:T(8,128)(2,1)S(1)}, bf16[256,1024]{1,0:T(8,128)(2,1)S(1)}, u32[]{:S(2)}, u32[]{:S(2)}) collective-permute-start(bf16[256,1024]{1,0:T(8,128)(2,1)S(1)} %convert_element_type.591), channel_id=1, source_target_pairs={{0,1},{1,2},{2,3},{3,0},{4,5},{5,6},{6,7},{7,4},{8,9},{9,10},{10,1... | collective-permute-start | bytes 1572872 | tf_op jit(solution)/shard_map/while/body/eval_jaxpr/ppermute | solution.py:17
  848.5 25.6 %collective-permute-start.5 = (bf16[256,1024]{1,0:T(8,128)(2,1)S(1)}, bf16[256,1024]{1,0:T(8,128)(2,1)S(1)}, u32[]{:S(2)}, u32[]{:S(2)}) collective-permute-start(bf16[256,1024]{1,0:T(8,128)(2,1)S(1)} %convert_element_type.591), channel_id=1, source_target_pairs={{0,3},{1,0},{2,1},{3,2},{4,7},{5,4},{6,5},{7,6},{8,11},{9,8},{10,9... | collective-permute-start | bytes 1572872 | tf_op jit(solution)/shard_map/while/body/eval_jaxpr/ppermute | solution.py:19
  862.7 21.1 %collective-permute-start.4 = (bf16[256,1024]{1,0:T(8,128)(2,1)S(1)}, bf16[256,1024]{1,0:T(8,128)(2,1)}, u32[]{:S(2)}, u32[]{:S(2)}) collective-permute-start(bf16[256,1024]{1,0:T(8,128)(2,1)S(1)} %collective-permute-done.3), channel_id=1, source_target_pairs={{0,1},{1,2},{2,3},{3,0},{4,5},{5,6},{6,7},{7,4},{8,9},{9,10},{10,1... | collective-permute-start | bytes 1572872 | tf_op jit(solution)/shard_map/while/body/eval_jaxpr/ppermute | solution.py:17
  874.1 134.9 %reduce-scatter.21.cloned.1.call-start = ((), (), s32[]{:S(2)}) async-start(), calls=%async_computation.19 | async-start | bytes 2621440 | tf_op jit(solution)/shard_map/while/body/eval_jaxpr/reduce_scatter | solution.py:123
  1017.6 56.4 %reduce-scatter.11.cloned.1.call-start = ((), (), s32[]{:S(2)}) async-start(), calls=%async_computation.9 | async-start | bytes 589824 | tf_op jit(solution)/shard_map/reduce_scatter | solution.py:319
  1019.8 76.8 %reduce-scatter.9.cloned.1.call-start = ((), (), s32[]{:S(2)}) async-start(), calls=%async_computation.8 | async-start | bytes 1769472 | tf_op jit(solution)/shard_map/reduce_scatter | solution.py:316
  1023.0 117.8 %reduce-scatter.13.cloned.1.call-start = ((), (), s32[]{:S(2)}) async-start(), calls=%async_computation.10 | async-start | bytes 2359296 | tf_op jit(solution)/shard_map/reduce_scatter | solution.py:322
  1027.0 158.1 %reduce-scatter.15.cloned.1.call-start = ((), (), s32[]{:S(2)}) async-start(), calls=%async_computation.11 | async-start | bytes 2359296 | tf_op jit(solution)/shard_map/reduce_scatter | solution.py:325
  (142 other events, 1351.7 us)
Sparse Core Ops, SparseCore 0:
  15.0 29.6 all-gather.7
  46.8 45.6 all-gather.5
  134.4 42.4 reduce-scatter.16
  178.6 26.9 all-gather.11
  207.6 47.4 all-gather.9
  256.9 26.2 all-gather.13
  296.9 43.6 reduce-scatter.18
  374.8 44.2 reduce-scatter.22
  467.7 41.7 reduce-scatter.20
  517.9 26.0 all-gather.7
  546.2 45.6 all-gather.5
  633.8 42.4 reduce-scatter.16
  678.2 26.9 all-gather.11
  707.2 47.3 all-gather.9
  756.3 26.2 all-gather.13
  796.3 43.6 reduce-scatter.18
  874.2 44.2 reduce-scatter.22
  967.1 41.7 reduce-scatter.20
Sparse Core Ops, SparseCore 1:
  1021.7 33.4 reduce-scatter.10
  1058.3 38.2 reduce-scatter.8
  1099.8 41.0 reduce-scatter.12
  1144.1 41.0 reduce-scatter.14
